TPU v7x, 32 devices: a whole 2x2x4 slice. The times are simulated.
32 devices in a mesh: dp: 16 (over z, y, core), tensor: 2 (over x).
Axes of the slice: x: 2, y: 2, z: 4, core: 2. Of those that a mesh axis runs over, the one named last changes fastest.
Arguments:
- patches: bfloat16 [37632, 768], P(('dp', 'tensor')), may hold values from -6 to 6
- gain_first: bfloat16 [768], replicated, may hold values from 0.099609375 to 1.8984375
- shift_first: bfloat16 [768], replicated, may hold values from -3 to 3
- attend_weight: bfloat16 [768, 2304], P(None, 'tensor'), may hold values from -0.21875 to 0.21875
- attend_bias: bfloat16 [24, 2, 32], P('tensor'), may hold values from -3 to 3
- offset_table: bfloat16 [24, 169], P('tensor'), may hold values from -5 to 5
- output_weight: bfloat16 [768, 768], P('tensor'), may hold values from -0.625 to 0.625
- output_bias: bfloat16 [768], replicated, may hold values from -3 to 3
- gain_second: bfloat16 [768], replicated, may hold values from 0.099609375 to 1.8984375
- shift_second: bfloat16 [768], replicated, may hold values from -3 to 3
- expand_weight: bfloat16 [768, 3072], P(None, 'tensor'), may hold values from -0.21875 to 0.21875
- expand_bias: bfloat16 [3072], P('tensor'), may hold values from -3 to 3
- reduce_weight: bfloat16 [3072, 768], P('tensor'), may hold values from -0.109375 to 0.109375
- reduce_bias: bfloat16 [768], replicated, may hold values from -3 to 3
- crop_counts: int32 [96], P('dp'), may hold values from 2 to 10, as said below
- cotangent: bfloat16 [37632, 768], P(('dp', 'tensor')), may hold values from -6 to 6
Outputs:
- result: bfloat16 [37632, 768], P(('dp', 'tensor'))
- input_grad: float32 [37632, 768], P(('dp', 'tensor'))
- gain_first_grad: float32 [768], P('tensor')
- shift_first_grad: float32 [768], P('tensor')
- attend_weight_grad: float32 [768, 2304], P(None, 'tensor')
- attend_bias_grad: float32 [24, 2, 32], P('tensor')
- offset_table_grad: float32 [24, 169], P('tensor')
- output_weight_grad: float32 [768, 768], P('tensor')
- output_bias_grad: float32 [768], P('tensor')
- gain_second_grad: float32 [768], P('tensor')
- shift_second_grad: float32 [768], P('tensor')
- expand_weight_grad: float32 [768, 3072], P(None, 'tensor')
- expand_bias_grad: float32 [3072], P('tensor')
- reduce_weight_grad: float32 [3072, 768], P('tensor')
- reduce_bias_grad: float32 [768], P('tensor')
Inputs may be any that keep to these rules, and one draw needn't show every extreme that they name: `crop_counts`: in each index of dp the counts of its 6 images sum to exactly 36, so their 2 + count windows fill its 48 window slots in order.
All inputs are finite; a program needn't handle non-finite values.
Results may differ from a plain program's by a relative error of at most 0.02.
Values may be sent and summed in bfloat16 or wider, within the bound.
No kernel may reach another device: no remote copies, remote signals or barrier semaphores. Data moves between devices by JAX's collectives and lax.ppermute only.
A program may use at most 256 MiB of HBM per device.

v0:
```python
from functools import partial
import jax
import jax.numpy as jnp
from jax import lax
from jax.sharding import PartitionSpec as P

HEAD_DIM = 32
HIGH = lax.Precision.HIGHEST
EPSILON = 1e-05
MASKED = 30000.0
SIDE = 7


def window_live(counts, slots):
    totals = counts + 2
    ends = jnp.cumsum(totals, dtype=jnp.int32)
    starts = ends - totals
    places = jnp.arange(slots, dtype=jnp.int32)[:, None]
    inside = (places >= starts[None, :]) & (places < ends[None, :])
    offset = jnp.sum(jnp.where(inside, places - starts[None, :], 0), axis=1, dtype=jnp.int32)
    present = jnp.any(inside, axis=1)
    spots = jnp.arange(SIDE * SIDE, dtype=jnp.int32)
    corner = (spots // SIDE < 3) & (spots % SIDE < 3)
    whole = present & (offset < 2)
    partial_win = present & (offset >= 2)
    alive = whole[:, None] | partial_win[:, None] & corner[None, :]
    return alive.astype(jnp.float32)


def offset_selector():
    spots = jnp.arange(SIDE * SIDE, dtype=jnp.int32)
    row_of = spots // SIDE
    col_of = spots % SIDE
    index = (
        (row_of[:, None] - row_of[None, :] + SIDE - 1) * (2 * SIDE - 1)
        + col_of[:, None]
        - col_of[None, :]
        + SIDE
        - 1
    )
    codes = jnp.arange((2 * SIDE - 1) ** 2, dtype=jnp.int32)
    return (codes[:, None] == index.reshape(1, -1)).astype(jnp.float32)


def norm_rows(values, gain, shift):
    mean = jnp.mean(values, axis=1, keepdims=True)
    centred = values - mean
    scale = lax.rsqrt(jnp.mean(centred * centred, axis=1, keepdims=True) + EPSILON)
    normal = centred * scale
    return (normal * gain + shift, normal, scale)


def norm_back(grad, normal, scale, gain):
    gain_grad = jnp.sum(grad * normal, axis=0)
    shift_grad = jnp.sum(grad, axis=0)
    inner = grad * gain
    centred = inner - jnp.mean(inner, axis=1, keepdims=True)
    return (
        scale * (centred - normal * jnp.mean(inner * normal, axis=1, keepdims=True)),
        gain_grad,
        shift_grad,
    )


def tdot(left, right):
    return lax.dot_general(
        left, right, (((0,), (0,)), ((), ())), preferred_element_type=jnp.float32
    )


def rdot(left, right):
    return lax.dot_general(
        left, right, (((1,), (1,)), ((), ())), preferred_element_type=jnp.float32
    )


def split_parts(block):
    query = (block[..., 0, :] * HEAD_DIM ** (-0.5)).astype(jnp.bfloat16)
    return (query, block[..., 1, :].astype(jnp.bfloat16), block[..., 2, :].astype(jnp.bfloat16))


def score_block(query, key, relative, mask):
    scores = jnp.einsum("wihd,wjhd->whij", query, key, preferred_element_type=jnp.float32)
    return scores + relative[None] + mask[:, None, None, :]


def block_layout(alive):
    windows = alive.shape[0]
    group = 8 if windows % 8 == 0 else windows
    return (windows, group, windows // group)


def attend_forward(packed, relative, alive, heads):
    windows, group, blocks = block_layout(alive)
    slots = SIDE * SIDE
    tiles = packed.reshape(blocks, group, slots, heads, 3, HEAD_DIM)
    masks = ((alive - 1.0) * MASKED).reshape(blocks, group, slots)

    def one(args):
        tile, mask = args
        query, key, value = split_parts(tile)
        scores = score_block(query, key, relative, mask)
        peak = jnp.max(scores, axis=3, keepdims=True)
        expo = jnp.exp(scores - peak)
        total = jnp.sum(expo, axis=3, keepdims=True)
        probs = (expo / total).astype(jnp.bfloat16)
        mixed = jnp.einsum("whij,wjhd->wihd", probs, value, preferred_element_type=jnp.float32)
        return (
            mixed.astype(jnp.bfloat16).reshape(group * slots, heads * HEAD_DIM),
            (peak + jnp.log(total))[..., 0],
        )

    mixed, norms = lax.map(one, (tiles, masks))
    return (mixed.reshape(windows * slots, heads * HEAD_DIM), norms)


def attend_backward(packed, mixed_grad, norms, relative, alive, heads):
    windows, group, blocks = block_layout(alive)
    slots = SIDE * SIDE
    tiles = packed.reshape(blocks, group, slots, heads, 3, HEAD_DIM)
    grads = mixed_grad.reshape(blocks, group, slots, heads, HEAD_DIM)
    masks = ((alive - 1.0) * MASKED).reshape(blocks, group, slots)

    def one(carry, args):
        tile, grad, mask, norm = args
        query, key, value = split_parts(tile)
        scores = score_block(query, key, relative, mask)
        soft = jnp.exp(scores - norm[..., None])
        probs = soft.astype(jnp.bfloat16)
        prob_grad = jnp.einsum("wihd,wjhd->whij", grad, value, preferred_element_type=jnp.float32)
        value_grad = jnp.einsum("whij,wihd->wjhd", probs, grad, preferred_element_type=jnp.float32)
        score_grad = soft * (prob_grad - jnp.sum(soft * prob_grad, axis=3, keepdims=True))
        score_grad = score_grad.astype(jnp.bfloat16)
        query_grad = jnp.einsum(
            "whij,wjhd->wihd", score_grad, key, preferred_element_type=jnp.float32
        )
        key_grad = jnp.einsum(
            "whij,wihd->wjhd", score_grad, query, preferred_element_type=jnp.float32
        )
        stacked = jnp.stack([query_grad * HEAD_DIM ** (-0.5), key_grad, value_grad], axis=3)
        stacked = stacked.astype(jnp.bfloat16).reshape(group * slots, heads * 3 * HEAD_DIM)
        return (carry + jnp.sum(score_grad.astype(jnp.float32), axis=0), stacked)

    start = jnp.zeros((heads, slots, slots), jnp.float32)
    table_grad, packed_grad = lax.scan(one, start, (tiles, grads, masks, norms))
    return (table_grad, packed_grad.reshape(windows * slots, heads * 3 * HEAD_DIM))


def on_device(
    patches,
    gain_first,
    shift_first,
    attend_weight,
    attend_bias,
    offset_table,
    output_weight,
    output_bias,
    gain_second,
    shift_second,
    expand_weight,
    expand_bias,
    reduce_weight,
    reduce_bias,
    crop_counts,
    cotangent,
):
    slots = SIDE * SIDE
    local_rows = patches.shape[0]
    local_windows = local_rows // slots
    group_live = window_live(crop_counts, crop_counts.shape[0] * 8)
    own_live = lax.dynamic_slice_in_dim(
        group_live, lax.axis_index("tensor") * local_windows, local_windows, 0
    )
    keep = own_live.reshape(local_rows, 1)
    inputs = patches.astype(jnp.float32)
    gain_one = gain_first.astype(jnp.float32)
    gain_two = gain_second.astype(jnp.float32)
    first, normal_one, scale_one = norm_rows(inputs, gain_one, shift_first.astype(jnp.float32))
    first = first.astype(jnp.bfloat16)
    w_attend, b_attend, t_offset, w_output, w_expand, b_expand, w_reduce = (
        lax.all_gather(attend_weight, "tensor", axis=1, tiled=True),
        lax.all_gather(attend_bias, "tensor", axis=0, tiled=True),
        lax.all_gather(offset_table, "tensor", axis=0, tiled=True),
        lax.all_gather(output_weight, "tensor", axis=0, tiled=True),
        lax.all_gather(expand_weight, "tensor", axis=1, tiled=True),
        lax.all_gather(expand_bias, "tensor", axis=0, tiled=True),
        lax.all_gather(reduce_weight, "tensor", axis=0, tiled=True),
    )
    heads = b_attend.shape[0]
    blank = jnp.zeros_like(b_attend[:, 0])
    bias_row = (
        jnp.stack([b_attend[:, 0], blank, b_attend[:, 1]], axis=1).reshape(-1).astype(jnp.float32)
    )
    packed = jnp.dot(first, w_attend, preferred_element_type=jnp.float32) + bias_row
    selector = offset_selector()
    relative = jnp.dot(t_offset.astype(jnp.float32), selector, precision=HIGH).reshape(
        heads, slots, slots
    )
    mixed, norms = attend_forward(packed, relative, own_live, heads)
    attended = jnp.dot(mixed, w_output, preferred_element_type=jnp.float32)
    middle = inputs + keep * (attended + output_bias.astype(jnp.float32))
    second, normal_two, scale_two = norm_rows(middle, gain_two, shift_second.astype(jnp.float32))
    second = second.astype(jnp.bfloat16)
    hidden_pre = jnp.dot(second, w_expand, preferred_element_type=jnp.float32) + b_expand.astype(
        jnp.float32
    )
    hidden = jax.nn.gelu(hidden_pre, approximate=False).astype(jnp.bfloat16)
    reduced = jnp.dot(hidden, w_reduce, preferred_element_type=jnp.float32)
    result = (middle + keep * (reduced + reduce_bias.astype(jnp.float32))).astype(jnp.bfloat16)
    upstream = cotangent.astype(jnp.float32)
    kept_up = keep * upstream
    reduce_bias_grad = jnp.sum(kept_up, axis=0)
    branch_grad = kept_up.astype(jnp.bfloat16)
    reduce_grad = tdot(hidden, branch_grad)
    hidden_grad = rdot(branch_grad, w_reduce)
    gelu_value, gelu_pull = jax.vjp(partial(jax.nn.gelu, approximate=False), hidden_pre)
    pre_grad = gelu_pull(hidden_grad)[0].astype(jnp.bfloat16)
    expand_grad = tdot(second, pre_grad)
    expand_bias_grad = jnp.sum(pre_grad.astype(jnp.float32), axis=0)
    second_grad = rdot(pre_grad, w_expand)
    middle_back, gain_two_grad, shift_two_grad = norm_back(
        second_grad, normal_two, scale_two, gain_two
    )
    middle_grad = upstream + middle_back
    kept_mid = keep * middle_grad
    output_bias_grad = jnp.sum(kept_mid, axis=0)
    attended_grad = kept_mid.astype(jnp.bfloat16)
    output_grad = tdot(mixed, attended_grad)
    mixed_grad = rdot(attended_grad, w_output).astype(jnp.bfloat16)
    relative_grad, packed_grad = attend_backward(
        packed, mixed_grad, norms, relative, own_live, heads
    )
    offset_grad = lax.dot_general(
        relative_grad.reshape(heads, slots * slots),
        selector,
        (((1,), (1,)), ((), ())),
        precision=HIGH,
    )
    attend_grad = tdot(first, packed_grad)
    packed_sum = jnp.sum(packed_grad.astype(jnp.float32), axis=0).reshape(heads, 3, HEAD_DIM)
    attend_bias_grad = jnp.stack([packed_sum[:, 0], packed_sum[:, 2]], axis=1)
    first_grad = rdot(packed_grad, w_attend)
    input_back, gain_one_grad, shift_one_grad = norm_back(
        first_grad, normal_one, scale_one, gain_one
    )
    input_grad = middle_grad + input_back
    small_grads = jnp.stack(
        [
            gain_one_grad,
            shift_one_grad,
            output_bias_grad,
            gain_two_grad,
            shift_two_grad,
            reduce_bias_grad,
        ]
    )
    (
        attend_grad,
        attend_bias_grad,
        offset_grad,
        output_grad,
        expand_grad,
        expand_bias_grad,
        reduce_grad,
        small_grads,
    ) = (
        lax.psum_scatter(
            attend_grad.astype(jnp.bfloat16), "tensor", scatter_dimension=1, tiled=True
        ).astype(jnp.float32),
        lax.psum_scatter(
            attend_bias_grad.astype(jnp.bfloat16), "tensor", scatter_dimension=0, tiled=True
        ).astype(jnp.float32),
        lax.psum_scatter(
            offset_grad.astype(jnp.bfloat16), "tensor", scatter_dimension=0, tiled=True
        ).astype(jnp.float32),
        lax.psum_scatter(
            output_grad.astype(jnp.bfloat16), "tensor", scatter_dimension=0, tiled=True
        ).astype(jnp.float32),
        lax.psum_scatter(
            expand_grad.astype(jnp.bfloat16), "tensor", scatter_dimension=1, tiled=True
        ).astype(jnp.float32),
        lax.psum_scatter(
            expand_bias_grad.astype(jnp.bfloat16), "tensor", scatter_dimension=0, tiled=True
        ).astype(jnp.float32),
        lax.psum_scatter(
            reduce_grad.astype(jnp.bfloat16), "tensor", scatter_dimension=0, tiled=True
        ).astype(jnp.float32),
        lax.psum_scatter(
            small_grads.astype(jnp.bfloat16), "tensor", scatter_dimension=1, tiled=True
        ).astype(jnp.float32),
    )
    totals = (
        lax.psum(attend_grad.astype(jnp.bfloat16), "dp").astype(jnp.float32),
        lax.psum(attend_bias_grad.astype(jnp.bfloat16), "dp").astype(jnp.float32),
        lax.psum(offset_grad.astype(jnp.bfloat16), "dp").astype(jnp.float32),
        lax.psum(output_grad.astype(jnp.bfloat16), "dp").astype(jnp.float32),
        lax.psum(expand_grad.astype(jnp.bfloat16), "dp").astype(jnp.float32),
        lax.psum(expand_bias_grad.astype(jnp.bfloat16), "dp").astype(jnp.float32),
        lax.psum(reduce_grad.astype(jnp.bfloat16), "dp").astype(jnp.float32),
        lax.psum(small_grads.astype(jnp.bfloat16), "dp").astype(jnp.float32),
    )
    smalls = totals[7]
    return (
        result,
        input_grad,
        smalls[0],
        smalls[1],
        totals[0],
        totals[1],
        totals[2],
        totals[3],
        smalls[2],
        smalls[3],
        smalls[4],
        totals[4],
        totals[5],
        totals[6],
        smalls[5],
    )


def solution(mesh):
    in_specs = (
        P(("dp", "tensor"), None),
        P(),
        P(),
        P(None, "tensor"),
        P("tensor", None, None),
        P("tensor", None),
        P("tensor", None),
        P(),
        P(),
        P(),
        P(None, "tensor"),
        P("tensor"),
        P("tensor", None),
        P(),
        P("dp"),
        P(("dp", "tensor"), None),
    )
    out_specs = (
        P(("dp", "tensor"), None),
        P(("dp", "tensor"), None),
        P("tensor"),
        P("tensor"),
        P(None, "tensor"),
        P("tensor", None, None),
        P("tensor", None),
        P("tensor", None),
        P("tensor"),
        P("tensor"),
        P("tensor"),
        P(None, "tensor"),
        P("tensor"),
        P("tensor", None),
        P("tensor"),
    )
    return jax.shard_map(
        on_device, mesh=mesh, in_specs=in_specs, out_specs=out_specs, check_vma=False
    )
```

profile of v0, /device:TPU:0, one launch (start us, length us, event | category | flops | bytes accessed | tf_op | source)
XLA Modules:
  0.0 892.9 jit_solution(10867279569873449285)
XLA Ops:
  12.0 5.3 all_gather.22
  17.8 4.4 all-gather
  24.6 4.6 all-gather.1
  30.2 31.6 %all-gather.7.cloned.1.call-done = bf16[768,2304]{1,0:T(8,128)(2,1)} async-done(((bf16[768,1152]{1,0:T(8,128)(2,1)}), bf16[768,2304]{1,0:T(8,128)(2,1)}) %all-gather.7.cloned.1.call-update) | async-done | bytes 3538960 | tf_op jit(solution)/shard_map/all_gather | solution.py:181
  61.8 9.5 %convolution_add_fusion = f32[1176,2304]{1,0:T(8,128)} fusion(bf16[768,2304]{1,0:T(8,128)(2,1)} %all-gather.7.cloned.1.call-done, f32[2304]{0:T(1024)S(1)} %reshape.292, bf16[1176,768]{1,0:T(8,128)(2,1)S(1)} %copy-done.4, f32[768]{0:T(1024)S(1)} %convert_element_type.189, f32[768]{0:T(1024)S(1)} %convert_element_type.188, f32[1176]{0:T(1024)S(1)} %add_rsqrt_fusion.1, ...), kind=kOutput, calls=%fused_computation.73 | convolution fusion | flops 4169926656 | bytes 16208064 | tf_op jit(solution)/shard_map/dot_general | solution.py:194
  71.3 13.2 %copy.92 = f32[1176,2304]{0,1:T(8,128)} copy(f32[1176,2304]{1,0:T(8,128)} %convolution_add_fusion) | data formatting | bytes 21676032 | tf_op jit(solution)/shard_map/add | solution.py:194
  84.5 23.0 %reshape.285 = f32[3,8,49,24,3,32]{2,1,0,5,4,3:T(8,128)} reshape(f32[1176,2304]{0,1:T(8,128)} %copy.92) | data formatting | bytes 21676032 | tf_op jit(solution)/shard_map/reshape | solution.py:96
  107.5 24.3 %copy.93 = f32[3,8,49,24,3,32]{2,5,3,1,4,0:T(8,128)} copy(f32[3,8,49,24,3,32]{2,1,0,5,4,3:T(8,128)} %reshape.285) | data formatting | bytes 21676032 | tf_op jit(solution)/shard_map/while | solution.py:113
  131.8 88.2 %while.25 = (s32[]{:T(128)}, bf16[3,392,768]{2,1,0:T(8,128)(2,1)}, f32[3,8,24,49]{3,2,1,0:T(8,128)}, f32[3,8,49,24,3,32]{2,5,3,1,4,0:T(8,128)}, f32[24,2401]{1,0...) while((s32[]{:T(128)}, bf16[3,392,768]{2,1,0:T(8,128)(2,1)}, f32[3,8,24,49]{3,2,1,0:T(8,128)}, ...), condition=%wide.region_8.9_spmd, body=%wide.region_5.8_spmd.sunk | while | flops 66335808 | bytes 27053972 | solution.py:113
  132.0 11.1 %fusion.121 = (bf16[8,49,24,3,32]{1,4,2,0,3:T(8,128)(2,1)}, f32[8,49,24,3,32]{1,4,2,0,3:T(8,128)}) fusion(f32[3,8,49,24,3,32]{2,5,3,1,4,0:T(8,128)} %get-tuple-element.399, s32[]{:T(128)} %get-tuple-element.389), kind=kLoop, calls=%fused_computation.158.clone.1 | loop fusion | flops 903168 | bytes 9031684 | tf_op jit(solution)/shard_map/convert.2
  143.7 4.6 fusion.122
  151.0 4.4 fusion.124
  155.3 3.4 copy.121
  161.1 11.9 %fusion.121 = (bf16[8,49,24,3,32]{1,4,2,0,3:T(8,128)(2,1)}, f32[8,49,24,3,32]{1,4,2,0,3:T(8,128)}) fusion(f32[3,8,49,24,3,32]{2,5,3,1,4,0:T(8,128)} %get-tuple-element.399, s32[]{:T(128)} %get-tuple-element.389), kind=kLoop, calls=%fused_computation.158.clone.1 | loop fusion | flops 903168 | bytes 9031684 | tf_op jit(solution)/shard_map/convert.2
  173.6 4.6 fusion.122
  180.8 4.4 fusion.124
  185.2 3.3 copy.121
  190.9 11.2 %fusion.121 = (bf16[8,49,24,3,32]{1,4,2,0,3:T(8,128)(2,1)}, f32[8,49,24,3,32]{1,4,2,0,3:T(8,128)}) fusion(f32[3,8,49,24,3,32]{2,5,3,1,4,0:T(8,128)} %get-tuple-element.399, s32[]{:T(128)} %get-tuple-element.389), kind=kLoop, calls=%fused_computation.158.clone.1 | loop fusion | flops 903168 | bytes 9031684 | tf_op jit(solution)/shard_map/convert.2
  202.7 4.6 fusion.122
  209.9 4.4 fusion.124
  214.3 3.3 copy.121
  220.0 4.4 fusion.84
  226.8 40.9 %multiply_convert_fusion.2 = (bf16[1176,3072]{1,0:T(8,128)(2,1)}, f32[1176,3072]{1,0:T(8,128)}, f32[1176,3072]{1,0:T(8,128)}) fusion(f32[3072]{0:T(1024)S(1)} %bitcast.161, bf16[768,3072]{1,0:T(8,128)(2,1)} %all-gather.11.cloned.1.call-done, f32[1176,768]{1,0:T(8,128)} %copy-done.6, f32[768]{0:T(1024)S(1)} %copy-done.37, f32[768]{0:T(1024)S(1)} %copy-done.25, ...), kind=kOutput, calls=%fused_computation.59 | convolution fusion | flops 5792016384 | bytes 44485824 | tf_op jit(solution)/shard_map/dot_general | solution.py:204
  267.8 19.7 %fusion.85 = (bf16[3072]{0:T(1024)(128)(2,1)}, bf16[1176,3072]{1,0:T(8,128)(2,1)}) fusion(f32[1176,3072]{1,0:T(8,128)} %get-tuple-element.254, f32[1176,3072]{1,0:T(8,128)} %get-tuple-element.269, bf16[3072,768]{1,0:T(8,128)(2,1)} %all-gather.13.cloned.1.call-done, bf16[1176,768]{1,0:T(8,128)(2,1)S(1)} %copy-done.11, f32[1176]{0:T(1024)S(1)} %copy-done.21), kind=kOutput, calls=%fused_computation.164 | convolution fusion | flops 5605960704 | bytes 42662496 | tf_op jit(solution)/shard_map/dot_general | solution.py:72
  287.5 13.2 %multiply_reduce_fusion.1 = (bf16[768]{0:T(1024)(128)(2,1)}, f32[1176]{0:T(1024)S(1)}, f32[1176]{0:T(1024)S(1)}, bf16[768]{0:T(1024)(128)(2,1)}, f32[1176,768]{1,0:T(8,128)S(1)}) fusion(f32[1176,768]{1,0:T(8,128)} %copy-done.6, f32[1176]{0:T(1024)S(1)} %add_rsqrt_fusion, f32[1176]{0:T(1024)S(1)} %broadcast_multiply_fusion.4, f32[768]{0:T(1024)S(1)} %copy-done.25, ...), kind=kOutput, calls=%fused_computation.104 | convolution fusion | flops 5557188608 | bytes 19194240 | tf_op jit(solution)/shard_map/dot_general | solution.py:72
  306.9 6.8 reshape.302
  313.7 9.2 %copy.97 = bf16[3,8,49,24,32]{2,4,3,1,0:T(8,128)(2,1)} copy(bf16[3,8,49,24,32]{4,3,2,1,0:T(8,128)(2,1)} %reshape.302) | data formatting | bytes 3612672
  322.9 159.5 %while.26 = (s32[]{:T(128)}, f32[24,49,49]{1,2,0:T(8,128)}, bf16[3,392,2304]{1,2,0:T(8,128)(2,1)}, f32[3,8,49,24,3,32]{2,5,3,1,4,0:T(8,128)}, f32[24,2401]{1,0:T...) while((s32[]{:T(128)}, f32[24,49,49]{1,2,0:T(8,128)}, ...), condition=%wide.region_16.17_spmd.clone, body=%wide.region_13.16_spmd.clone.sunk | while | flops 160520480 | bytes 91262472 | solution.py:145
  323.0 7.6 fusion.131
  330.6 6.6 fusion.132
  339.4 6.5 multiply_reduce_fusion.8
  350.9 3.4 fusion.134
  358.7 7.6 copy.123
  366.3 6.4 convert_element_type.347
  375.3 7.6 fusion.131
  382.9 6.6 fusion.132
  391.7 6.5 multiply_reduce_fusion.8
  403.1 3.4 fusion.134
  410.9 7.6 copy.123
  418.5 6.4 convert_element_type.347
  428.6 7.7 fusion.131
  436.3 6.6 fusion.132
  445.1 6.5 multiply_reduce_fusion.8
  456.5 3.4 fusion.134
  464.3 7.6 copy.123
  471.9 6.4 convert_element_type.347
  482.4 9.2 %copy.98 = bf16[3,392,2304]{2,1,0:T(8,128)(2,1)} copy(bf16[3,392,2304]{1,2,0:T(8,128)(2,1)} %get-tuple-element.93) | data formatting | bytes 10838016 | tf_op jit(solution)/shard_map/while | solution.py:145
  491.6 9.2 %convolution_convert_fusion.3 = bf16[768,2304]{1,0:T(8,128)(2,1)} fusion(bf16[1176,2304]{1,0:T(8,128)(2,1)} %bitcast.156, bf16[1176,768]{1,0:T(8,128)(2,1)S(1)} %copy-done.5, f32[768]{0:T(1024)S(1)} %copy-done.40, f32[768]{0:T(1024)S(1)} %copy-done.28, f32[1176]{0:T(1024)S(1)} %copy-done.20, f32[1176]{0:T(1024)S(1)} %copy-done.16), kind=kOutput, calls=%fused_computation.80 | convolution fusion | flops 4168986624 | bytes 10779840 | tf_op jit(solution)/shard_map/dot_general | solution.py:66
  500.8 5.8 copy.108
  506.7 5.5 convolution_convert_fusion.5
  512.3 12.8 %convolution_convert_fusion.2 = bf16[768,3072]{1,0:T(8,128)(2,1)} fusion(bf16[1176,3072]{1,0:T(8,128)(2,1)} %get-tuple-element.273, f32[1176,768]{1,0:T(8,128)} %copy-done.6, f32[768]{0:T(1024)S(1)} %copy-done.38, f32[768]{0:T(1024)S(1)} %copy-done.26, f32[1176]{0:T(1024)S(1)} %copy-done.24, f32[1176]{0:T(1024)S(1)} %copy-done.18), kind=kOutput, calls=%fused_computation.79 | convolution fusion | flops 5555939328 | bytes 15572160 | tf_op jit(solution)/shard_map/dot_general | solution.py:66
  525.2 11.2 %convolution_convert_fusion.1 = bf16[3072,768]{1,0:T(8,128)(2,1)} fusion(bf16[1176,3072]{1,0:T(8,128)(2,1)} %get-tuple-element.253, bf16[1176,768]{1,0:T(8,128)(2,1)} %param.35, f32[1176]{0:T(1024)S(1)} %copy-done.22), kind=kOutput, calls=%fused_computation.78 | convolution fusion | flops 5554132992 | bytes 13754976 | tf_op jit(solution)/shard_map/dot_general | solution.py:66
  539.6 4.1 reduce.2
  545.3 5.9 fusion
  554.6 10.6 %fusion.65 = (bf16[768]{0:T(1024)(128)(2,1)S(1)}, f32[1176]{0:T(1024)S(1)}, f32[1176]{0:T(1024)S(1)}, bf16[768]{0:T(1024)(128)(2,1)S(1)}, f32[1176,768]{1,0:T(8,128)}) fusion(bf16[1176,768]{1,0:T(8,128)(2,1)S(1)} %copy-done.5, f32[1176]{0:T(1024)S(1)} %copy-done.20, f32[1176]{0:T(1024)S(1)} %copy-done.16, f32[768]{0:T(1024)S(1)} %copy-done.28, ...), kind=kOutput, calls=%fused_computation.102 | convolution fusion | flops 4170825728 | bytes 14401920 | tf_op jit(solution)/shard_map/dot_general | solution.py:72
  566.4 7.3 all-reduce.6
  573.7 3.9 copy.109
  579.9 62.9 %reduce-scatter.14.cloned.1.call-done = bf16[768,1536]{1,0:T(8,128)(2,1)} async-done(((bf16[768,3072]{1,0:T(8,128)(2,1)}), bf16[768,1536]{1,0:T(8,128)(2,1)}) %reduce-scatter.14.cloned.1.call-update) | async-done | bytes 2359312 | tf_op jit(solution)/shard_map/reduce_scatter | solution.py:279
  642.8 63.0 %reduce-scatter.16.cloned.1.call-done = bf16[1536,768]{1,0:T(8,128)(2,1)} async-done(((bf16[3072,768]{1,0:T(8,128)(2,1)}), bf16[1536,768]{1,0:T(8,128)(2,1)}) %reduce-scatter.16.cloned.1.call-update) | async-done | bytes 2359312 | tf_op jit(solution)/shard_map/reduce_scatter | solution.py:285
  705.8 5.2 fusion.64
  711.0 10.5 %fusion.67 = bf16[1176,768]{1,0:T(8,128)(2,1)} fusion(f32[1176,768]{1,0:T(8,128)S(1)} %copy-done.8, bf16[1176,3072]{1,0:T(8,128)(2,1)} %get-tuple-element.253, bf16[3072,768]{1,0:T(8,128)(2,1)} %all-gather.13.cloned.1.call-done, f32[768]{0:T(1024)S(1)} %convert_element_type.199, f32[1176]{0:T(1024)S(1)} %copy-done.22), kind=kOutput, calls=%fused_computation.111 | convolution fusion | flops 5552676864 | bytes 17370720 | tf_op jit(solution)/shard_map/dot_general | solution.py:208
  722.8 64.1 %all-reduce.4 = (bf16[6,384]{1,0:T(8,128)(2,1)S(1)}, bf16[12,2,32]{2,1,0:T(2,128)(2,1)S(1)}, bf16[12,169]{1,0:T(8,128)(2,1)S(1)}, bf16[1536]{0:T(1024)(128)(2,1)S(1)}) all-reduce(bf16[6,384]{1,0:T(8,128)(2,1)S(1)} %copy.107, bf16[12,2,32]{2,1,0:T(2,128)(2,1)S(1)} %constant_dynamic-slice_fusion.1, ...), channel_id=1, replica_groups=mesh['dp'=16,'tensor'=2] {'dp'}, use_global_device_ids=true, to_apply=%region_26.27 | all-reduce | flops 6636 | bytes 26544 | tf_op jit(solution)/shard_map/psum | solution.py:300
  789.3 86.3 %all-reduce.9.cloned.1.call-done = (bf16[768,1152]{1,0:T(8,128)(2,1)}, bf16[384,768]{1,0:T(8,128)(2,1)}, bf16[768,1536]{1,0:T(8,128)(2,1)}, bf16[1536,768]{1,0:T(8,128)(2,1)}) async-done(((bf16[768,1152]{1,0:T(8,128)(2,1)}, bf16[384,768]{1,0:T(8,128)(2,1)}, bf16[768,1536]{1,0:T(8,128)(2,1)}, bf16[1536,768]{1,0:T(8,128)(2,1)}), (bf16[768,1152]{1,0:T(8,128)(2,1)}, bf16[384,768]{1,0:T(8,128)(2,1)}, ...) | async-done | bytes 7077904 | tf_op jit(solution)/shard_map/psum | solution.py:293
  875.6 4.6 convert_element_type.216
  (281 shorter events, 97.2 us)
Async XLA Ops:
  7.2 2.9 copy-start.53
  7.2 3.7 copy-start.4
  7.2 54.6 %all-gather.7.cloned.1.call-start = ((), (), s32[]{:S(2)}) async-start(), calls=%async_computation.5 | async-start | bytes 5308416 | tf_op jit(solution)/shard_map/all_gather | solution.py:181
  7.9 212.1 %all-gather.9.cloned.1.call-start = ((), (), s32[]{:S(2)}) async-start(), calls=%async_computation.6 | async-start | bytes 1769472 | tf_op jit(solution)/shard_map/all_gather | solution.py:184
  8.7 218.1 %all-gather.11.cloned.1.call-start = ((), (), s32[]{:S(2)}) async-start(), calls=%async_computation.7 | async-start | bytes 7077888 | tf_op jit(solution)/shard_map/all_gather | solution.py:185
  9.4 8.1 copy-start.44
  9.5 8.3 copy-start.34
  9.5 13.4 %copy-start.45 = (bf16[768]{0:T(1024)(128)(2,1)S(1)}, bf16[768]{0:T(1024)(128)(2,1)}, u32[]{:S(2)}) copy-start(bf16[768]{0:T(1024)(128)(2,1)} %param.27) | copy-start | bytes 4612
  9.5 14.0 %copy-start.46 = (bf16[768]{0:T(1024)(128)(2,1)S(1)}, bf16[768]{0:T(1024)(128)(2,1)}, u32[]{:S(2)}) copy-start(bf16[768]{0:T(1024)(128)(2,1)} %param.28) | copy-start | bytes 4612
  9.5 14.5 %copy-start.47 = (bf16[768]{0:T(1024)(128)(2,1)S(1)}, bf16[768]{0:T(1024)(128)(2,1)}, u32[]{:S(2)}) copy-start(bf16[768]{0:T(1024)(128)(2,1)} %param.29) | copy-start | bytes 4612
  9.5 15.1 %copy-start.42 = (bf16[1536]{0:T(1024)(128)(2,1)S(1)}, bf16[1536]{0:T(1024)(128)(2,1)}, u32[]{:S(2)}) copy-start(bf16[1536]{0:T(1024)(128)(2,1)} %param.31) | copy-start | bytes 9220
  9.5 258.2 %all-gather.13.cloned.1.call-start = ((), (), s32[]{:S(2)}) async-start(), calls=%async_computation.8 | async-start | bytes 7077888 | tf_op jit(solution)/shard_map/all_gather | solution.py:187
  10.1 563.6 %reduce-scatter.20.cloned.1.call-start = ((), (), s32[]{:S(2)}) async-start(), calls=%async_computation.13 | async-start | bytes 5308416
  11.2 60.1 %copy-start.15 = (f32[1176]{0:T(1024)}, f32[1176]{0:T(1024)S(1)}, u32[]{:S(2)}) copy-start(f32[1176]{0:T(1024)S(1)} %broadcast_multiply_fusion.5) | copy-start | bytes 14116
  11.9 59.4 %copy-start.19 = (f32[1176]{0:T(1024)}, f32[1176]{0:T(1024)S(1)}, u32[]{:S(2)}) copy-start(f32[1176]{0:T(1024)S(1)} %add_rsqrt_fusion.1) | copy-start | bytes 14116
  12.0 59.3 %copy-start.27 = (f32[768]{0:T(1024)}, f32[768]{0:T(1024)S(1)}, u32[]{:S(2)}) copy-start(f32[768]{0:T(1024)S(1)} %convert_element_type.188) | copy-start | bytes 9220
  17.5 53.8 %copy-start.39 = (f32[768]{0:T(1024)}, f32[768]{0:T(1024)S(1)}, u32[]{:S(2)}) copy-start(f32[768]{0:T(1024)S(1)} %convert_element_type.189) | copy-start | bytes 9220
  17.7 53.6 %copy-start.30 = (s32[2401]{0:T(1024)}, s32[2401]{0:T(1024)S(1)}, u32[]{:S(2)}) copy-start(s32[2401]{0:T(1024)S(1)} %reshape.296) | copy-start | bytes 28816
  131.8 88.2 %copy-start.21 = (f32[1176]{0:T(1024)S(1)}, f32[1176]{0:T(1024)}, u32[]{:S(2)}) copy-start(f32[1176]{0:T(1024)} %mul.191) | copy-start | bytes 14116
  131.8 88.2 %copy-start.41 = (f32[768]{0:T(1024)S(1)}, f32[768]{0:T(1024)}, u32[]{:S(2)}) copy-start(f32[768]{0:T(1024)} %convert_element_type.193) | copy-start | bytes 9220
  220.0 4.4 copy-start.2
  220.0 4.4 copy-start.14
  224.5 76.2 %copy-start.17 = (f32[1176]{0:T(1024)}, f32[1176]{0:T(1024)S(1)}, u32[]{:S(2)}) copy-start(f32[1176]{0:T(1024)S(1)} %broadcast_multiply_fusion.4) | copy-start | bytes 14116
  226.8 73.9 %copy-start.23 = (f32[1176]{0:T(1024)}, f32[1176]{0:T(1024)S(1)}, u32[]{:S(2)}) copy-start(f32[1176]{0:T(1024)S(1)} %add_rsqrt_fusion) | copy-start | bytes 14116
  226.8 40.9 %copy-start.11 = (bf16[1176,768]{1,0:T(8,128)(2,1)S(1)}, bf16[1176,768]{1,0:T(8,128)(2,1)}, u32[]{:S(2)}) copy-start(bf16[1176,768]{1,0:T(8,128)(2,1)} %param.35) | copy-start | bytes 5419012
  287.5 13.2 %copy-start.7 = (f32[1176,768]{1,0:T(8,128)S(1)}, f32[1176,768]{1,0:T(8,128)}, u32[]{:S(2)}) copy-start(f32[1176,768]{1,0:T(8,128)} %copy-done.6) | copy-start | bytes 10838020
  300.7 4.5 copy-start.52
  313.7 9.2 %copy-start.3 = (f32[24,2401]{1,0:T(8,128)S(1)}, f32[24,2401]{1,0:T(8,128)}, u32[]{:S(2)}) copy-start(f32[24,2401]{1,0:T(8,128)} %copy-done.2) | copy-start | bytes 691492
  330.6 6.6 copy-start
  339.4 6.5 slice-start
  339.4 6.5 slice-start.1
  382.9 6.6 copy-start
  391.7 6.5 slice-start
  391.7 6.5 slice-start.1
  436.3 6.6 copy-start
  445.1 6.5 slice-start
  445.1 6.5 slice-start.1
  482.4 9.2 %copy-start.5 = (bf16[1176,768]{1,0:T(8,128)(2,1)S(1)}, bf16[1176,768]{1,0:T(8,128)(2,1)}, u32[]{:S(2)}) copy-start(bf16[1176,768]{1,0:T(8,128)(2,1)} %param.20) | copy-start | bytes 5419012
  482.4 9.2 %copy-start.16 = (f32[1176]{0:T(1024)S(1)}, f32[1176]{0:T(1024)}, u32[]{:S(2)}) copy-start(f32[1176]{0:T(1024)} %copy-done.15) | copy-start | bytes 14116
  482.4 9.2 %copy-start.20 = (f32[1176]{0:T(1024)S(1)}, f32[1176]{0:T(1024)}, u32[]{:S(2)}) copy-start(f32[1176]{0:T(1024)} %copy-done.19) | copy-start | bytes 14116
  482.4 9.2 %copy-start.28 = (f32[768]{0:T(1024)S(1)}, f32[768]{0:T(1024)}, u32[]{:S(2)}) copy-start(f32[768]{0:T(1024)} %copy-done.27) | copy-start | bytes 9220
  482.4 9.2 %copy-start.40 = (f32[768]{0:T(1024)S(1)}, f32[768]{0:T(1024)}, u32[]{:S(2)}) copy-start(f32[768]{0:T(1024)} %copy-done.39) | copy-start | bytes 9220
  500.8 5.9 copy-start.22
  506.6 5.7 copy-start.18
  506.6 5.7 copy-start.24
  506.6 5.7 copy-start.26
  506.6 5.7 copy-start.38
  506.6 73.2 %reduce-scatter.12.cloned.1.call-start = ((), (), s32[]{:S(2)}) async-start(), calls=%async_computation.9 | async-start | bytes 1769472 | tf_op jit(solution)/shard_map/reduce_scatter | solution.py:276
  512.2 130.6 %reduce-scatter.14.cloned.1.call-start = ((), (), s32[]{:S(2)}) async-start(), calls=%async_computation.10 | async-start | bytes 7077888 | tf_op jit(solution)/shard_map/reduce_scatter | solution.py:279
  525.2 180.6 %reduce-scatter.16.cloned.1.call-start = ((), (), s32[]{:S(2)}) async-start(), calls=%async_computation.11 | async-start | bytes 7077888 | tf_op jit(solution)/shard_map/reduce_scatter | solution.py:285
  536.4 3.2 copy-start.48
  536.4 7.3 copy-start.1
  536.5 185.3 %reduce-scatter.18.cloned.1.call-start = ((), (), s32[]{:S(2)}) async-start(), calls=%async_computation.12 | async-start | bytes 294912
  539.6 4.7 copy-start.31
  551.2 170.4 %collective-permute-start = (bf16[4,169]{1,0:T(4,128)(2,1)S(1)}, bf16[4,169]{1,0:T(4,128)(2,1)S(1)}, u32[]{:S(2)}, u32[]{:S(2)}) collective-permute-start(bf16[4,169]{1,0:T(4,128)(2,1)S(1)} %slice.83), channel_id=1, source_target_pairs={{0,1},{2,3},{4,5},{6,7},{8,9},{10,11},{12,13},{14,15},{16,17},{18,... | collective-permute-start | bytes 4064
  554.5 10.7 %copy-start.33 = (bf16[768]{0:T(1024)(128)(2,1)S(1)}, bf16[768]{0:T(1024)(128)(2,1)}, u32[]{:S(2)}) copy-start(bf16[768]{0:T(1024)(128)(2,1)} %get-tuple-element.207) | copy-start | bytes 4612
  554.5 10.7 %copy-start.32 = (bf16[768]{0:T(1024)(128)(2,1)S(1)}, bf16[768]{0:T(1024)(128)(2,1)}, u32[]{:S(2)}) copy-start(bf16[768]{0:T(1024)(128)(2,1)} %get-tuple-element.206) | copy-start | bytes 4612
  554.5 10.7 %copy-start.50 = (bf16[768]{0:T(1024)(128)(2,1)S(1)}, bf16[768]{0:T(1024)(128)(2,1)}, u32[]{:S(2)}) copy-start(bf16[768]{0:T(1024)(128)(2,1)} %get-tuple-element.192) | copy-start | bytes 4612
  554.5 10.7 %copy-start.49 = (bf16[768]{0:T(1024)(128)(2,1)S(1)}, bf16[768]{0:T(1024)(128)(2,1)}, u32[]{:S(2)}) copy-start(bf16[768]{0:T(1024)(128)(2,1)} %get-tuple-element.198) | copy-start | bytes 4612
  554.6 11.8 %copy-start.36 = (bf16[3072]{0:T(1024)(128)(2,1)S(1)}, bf16[3072]{0:T(1024)(128)(2,1)}, u32[]{:S(2)}) copy-start(bf16[3072]{0:T(1024)(128)(2,1)} %get-tuple-element.272) | copy-start | bytes 18436
  566.3 309.3 %all-reduce.9.cloned.1.call-start = ((), (), s32[]{:S(2)}) async-start(), calls=%async_computation.14 | async-start | bytes 14155776 | tf_op jit(solution)/shard_map/psum | solution.py:293
  705.8 5.2 copy-start.8
  875.6 4.7 copy-start.10
  880.2 2.6 copy-start.12
  (9 other events, 18.4 us)
Sparse Core Ops, SparseCore 0:
  9.6 52.1 all-gather.6
  63.4 22.8 all-gather.8
  87.8 62.6 all-gather.10
  151.9 62.6 all-gather.12
  506.7 48.0 reduce-scatter.19
  557.5 22.2 reduce-scatter.11
  582.8 59.9 reduce-scatter.13
  645.8 59.9 reduce-scatter.15
  708.0 10.9 reduce-scatter.17
  723.5 152.0 all-reduce.8
where the time goes:
time: 902 us; the launch traced here: 893 us
  waiting for transfers between devices  249 us (28%)
  matrix products  243 us (27%)
  local copies, waits for them, and re-layouts  177 us (20%)
  other arithmetic  110 us (12%)
  blocking collectives  91.5 us (10%)
  between operations  17.2 us (2%)
    psum x1, waiting for transfers between devices, on_device(): lax.psum(attend_grad.astype(jnp.bfloat16), 'dp').astype(jnp.float32)  86.3 us
    psum x1, blocking collectives, on_device(): lax.psum(small_grads.astype(jnp.bfloat16), 'dp').astype(jnp.float32)  64.1 us
    reduce_scatter x1, waiting for transfers between devices, on_device(): lax.psum_scatter(reduce_grad.astype(jnp.bfloat16), 'tensor', scatter_dime...  63 us
    reduce_scatter x1, waiting for transfers between devices, on_device(): lax.psum_scatter(expand_grad.astype(jnp.bfloat16), 'tensor', scatter_dime...  62.9 us
    another operation x8, other arithmetic  57.1 us
    dot_general x4, matrix products, rdot(): lax.dot_general(left, right, (((1,), (1,)), ((), ())), preferred_element_...  45.2 us
    dot_general x1, matrix products, on_device(): jnp.dot(second, w_expand, preferred_element_type=jnp.float32)  40.9 us
    dot_general x4, matrix products, tdot(): lax.dot_general(left, right, (((0,), (0,)), ((), ())), preferred_element_...  38.7 us
  transfers between devices with their start and end apart: 11, of which 5 were waited for; matrix products, arithmetic and copies ran while one was open for 32% of the time, Pallas kernels for 0%

commit v1 on v0

--- a/solution.py
+++ b/solution.py
@@ -9,6 +9,12 @@
 EPSILON = 1e-05
 MASKED = 30000.0
 SIDE = 7
+
+
+def summed_here(x, axis):
+    blocks = lax.all_gather(x, axis, axis=0, tiled=False)
+    total = blocks.sum(axis=0)
+    return total
 
 
 def window_live(counts, slots):
@@ -290,7 +296,7 @@
         ).astype(jnp.float32),
     )
     totals = (
-        lax.psum(attend_grad.astype(jnp.bfloat16), "dp").astype(jnp.float32),
+        summed_here(attend_grad.astype(jnp.bfloat16), "dp").astype(jnp.float32),
         lax.psum(attend_bias_grad.astype(jnp.bfloat16), "dp").astype(jnp.float32),
         lax.psum(offset_grad.astype(jnp.bfloat16), "dp").astype(jnp.float32),
         lax.psum(output_grad.astype(jnp.bfloat16), "dp").astype(jnp.float32),

time: 902 us -> 865 us (0.959)
  matrix products: 243 us -> 213 us
    all_gather x0 -> x1, waiting for transfers between devices: none -> 136 us  [summed_here(): blocks = lax.all_gather(x, axis, axis=0, tiled=False)]
    reduce_scatter x1, waiting for transfers between devices: 63 us -> 0.02 us  [on_device(): lax.psum_scatter(reduce_grad.astype(jnp.bfloat16), 'tensor', scatter_dime...]
    reduce_scatter x1, waiting for transfers between devices: 62.9 us -> 0.02 us  [on_device(): lax.psum_scatter(expand_grad.astype(jnp.bfloat16), 'tensor', scatter_dime...]
    psum x1, waiting for transfers between devices: 86.3 us -> 36.2 us  [on_device(): lax.psum(output_grad.astype(jnp.bfloat16), 'dp').astype(jnp.float32)]
    unnamed x13 -> x14, waiting for transfers between devices: 2.7 us -> 39.3 us
    dot_general x6, matrix products: 33.6 us -> 21.1 us  [score_block(): jnp.einsum('wihd,wjhd->whij', query, key, preferred_element_type=jnp.floa...]
    reduce_sum x0 -> x1, other arithmetic: none -> 10.1 us  [summed_here(): total = blocks.sum(axis=0)]
    another operation x8, other arithmetic: 57.1 us -> 47.4 us
  transfers between devices with their start and end apart: 11 -> 12, of which waited for: 5 -> 4; matrix products, arithmetic and copies ran while one was open for 32% -> 53% of each run, Pallas kernels for 0% -> 0%
where the time goes in v1:
time: 865 us; the launch traced here: 856 us
  waiting for transfers between devices  244 us (28%)
  matrix products  213 us (25%)
  local copies, waits for them, and re-layouts  184 us (21%)
  other arithmetic  107 us (12%)
  blocking collectives  85.3 us (10%)
  between operations  16.8 us (2%)
    all_gather x1, waiting for transfers between devices, summed_here(): blocks = lax.all_gather(x, axis, axis=0, tiled=False)  136 us
    psum x1, blocking collectives, on_device(): lax.psum(small_grads.astype(jnp.bfloat16), 'dp').astype(jnp.float32)  58.9 us
    another operation x8, other arithmetic  47.4 us
    dot_general x4, matrix products, rdot(): lax.dot_general(left, right, (((1,), (1,)), ((), ())), preferred_element_...  46.9 us
    dot_general x1, matrix products, on_device(): jnp.dot(second, w_expand, preferred_element_type=jnp.float32)  41 us
    unnamed x14, waiting for transfers between devices  39.3 us
    dot_general x4, matrix products, tdot(): lax.dot_general(left, right, (((0,), (0,)), ((), ())), preferred_element_...  36.3 us
    psum x1, waiting for transfers between devices, on_device(): lax.psum(output_grad.astype(jnp.bfloat16), 'dp').astype(jnp.float32)  36.2 us
  transfers between devices with their start and end apart: 12, of which 4 were waited for; matrix products, arithmetic and copies ran while one was open for 53% of the time, Pallas kernels for 0%

profile of v1, /device:TPU:0, one launch (start us, length us, event | category | flops | bytes accessed | tf_op | source)
XLA Modules:
  0.0 855.9 jit_solution(4179992797308479750)
XLA Ops:
  12.7 5.3 all-gather.2
  20.3 4.3 all_gather.28
  24.7 4.6 all-gather.1
  30.2 31.8 %all-gather.9.cloned.1.call-done = bf16[768,2304]{1,0:T(8,128)(2,1)} async-done(((bf16[768,1152]{1,0:T(8,128)(2,1)}), bf16[768,2304]{1,0:T(8,128)(2,1)}) %all-gather.9.cloned.1.call-update) | async-done | bytes 3538960 | tf_op jit(solution)/shard_map/all_gather | solution.py:187
  62.0 9.5 %convolution_add_fusion = f32[1176,2304]{1,0:T(8,128)} fusion(bf16[768,2304]{1,0:T(8,128)(2,1)} %all-gather.9.cloned.1.call-done, f32[2304]{0:T(1024)S(1)} %reshape.292, bf16[1176,768]{1,0:T(8,128)(2,1)S(1)} %copy-done.8, f32[768]{0:T(1024)S(1)} %convert_element_type.191, f32[768]{0:T(1024)S(1)} %convert_element_type.190, f32[1176]{0:T(1024)S(1)} %add_rsqrt_fusion.1, ...), kind=kOutput, calls=%fused_computation.73 | convolution fusion | flops 4169926656 | bytes 16208064 | tf_op jit(solution)/shard_map/dot_general | solution.py:200
  71.5 13.2 %copy.92 = f32[1176,2304]{0,1:T(8,128)} copy(f32[1176,2304]{1,0:T(8,128)} %convolution_add_fusion) | data formatting | bytes 21676032 | tf_op jit(solution)/shard_map/add | solution.py:200
  84.7 23.0 %reshape.285 = f32[3,8,49,24,3,32]{2,1,0,5,4,3:T(8,128)} reshape(f32[1176,2304]{0,1:T(8,128)} %copy.92) | data formatting | bytes 21676032 | tf_op jit(solution)/shard_map/reshape | solution.py:102
  107.7 24.3 %copy.93 = f32[3,8,49,24,3,32]{2,5,3,1,4,0:T(8,128)} copy(f32[3,8,49,24,3,32]{2,1,0,5,4,3:T(8,128)} %reshape.285) | data formatting | bytes 21676032 | tf_op jit(solution)/shard_map/while | solution.py:119
  132.0 78.2 %while.25 = (s32[]{:T(128)}, bf16[3,392,768]{2,1,0:T(8,128)(2,1)}, f32[3,8,24,49]{3,2,1,0:T(8,128)}, f32[3,8,49,24,3,32]{2,5,3,1,4,0:T(8,128)}, f32[24,2401]{1,0...) while((s32[]{:T(128)}, bf16[3,392,768]{2,1,0:T(8,128)(2,1)}, f32[3,8,24,49]{3,2,1,0:T(8,128)}, ...), condition=%wide.region_8.9_spmd, body=%wide.region_5.8_spmd.sunk | while | flops 66335808 | bytes 28435136 | solution.py:119
  133.6 7.6 fusion.121
  141.2 3.9 fusion.122
  147.1 4.3 fusion.124
  152.1 3.3 copy.122
  159.3 8.6 %fusion.121 = (bf16[8,49,24,3,32]{1,4,2,0,3:T(8,128)(2,1)}, f32[8,49,24,3,32]{1,4,2,0,3:T(8,128)S(1)}) fusion(f32[3,8,49,24,3,32]{2,5,3,1,4,0:T(8,128)} %get-tuple-element.398, s32[]{:T(128)S(6)} %copy.131), kind=kLoop, calls=%fused_computation.158.clone.1 | loop fusion | flops 903168 | bytes 9031684 | tf_op jit(solution)/shard_map/convert.3
  167.9 3.9 fusion.122
  173.7 4.3 fusion.124
  178.8 3.3 copy.122
  185.9 7.7 fusion.121
  193.6 3.9 fusion.122
  199.4 4.3 fusion.124
  204.4 3.3 copy.122
  210.2 4.3 fusion.84
  217.0 41.0 %multiply_convert_fusion.2 = (bf16[1176,3072]{1,0:T(8,128)(2,1)}, f32[1176,3072]{1,0:T(8,128)}, f32[1176,3072]{1,0:T(8,128)}) fusion(f32[3072]{0:T(1024)S(1)} %bitcast.161, bf16[768,3072]{1,0:T(8,128)(2,1)} %all-gather.13.cloned.1.call-done, f32[1176,768]{1,0:T(8,128)} %copy-done.10, f32[768]{0:T(1024)S(1)} %copy-done.36, f32[768]{0:T(1024)S(1)} %copy-done.23, ...), kind=kOutput, calls=%fused_computation.59 | convolution fusion | flops 5792016384 | bytes 44485824 | tf_op jit(solution)/shard_map/dot_general | solution.py:210
  258.0 19.4 %fusion.85 = (bf16[3072]{0:T(1024)(128)(2,1)}, bf16[1176,3072]{1,0:T(8,128)(2,1)}) fusion(f32[1176,3072]{1,0:T(8,128)} %get-tuple-element.253, f32[1176,3072]{1,0:T(8,128)} %get-tuple-element.268, bf16[3072,768]{1,0:T(8,128)(2,1)} %all-gather.15.cloned.1.call-done, bf16[1176,768]{1,0:T(8,128)(2,1)S(1)} %copy-done.15, f32[1176]{0:T(1024)S(1)} %copy-done.19), kind=kOutput, calls=%fused_computation.164 | convolution fusion | flops 5605960704 | bytes 42662496 | tf_op jit(solution)/shard_map/dot_general | solution.py:78
  277.5 13.2 %multiply_reduce_fusion.1 = (bf16[768]{0:T(1024)(128)(2,1)}, f32[1176]{0:T(1024)S(1)}, f32[1176]{0:T(1024)S(1)}, bf16[768]{0:T(1024)(128)(2,1)}, f32[1176,768]{1,0:T(8,128)S(1)}) fusion(f32[1176,768]{1,0:T(8,128)} %copy-done.10, f32[1176]{0:T(1024)S(1)} %add_rsqrt_fusion, f32[1176]{0:T(1024)S(1)} %broadcast_multiply_fusion.4, f32[768]{0:T(1024)S(1)} %copy-done.23, ...), kind=kOutput, calls=%fused_computation.104 | convolution fusion | flops 5557188608 | bytes 19194240 | tf_op jit(solution)/shard_map/dot_general | solution.py:78
  298.3 12.1 %convolution_convert_fusion.1 = bf16[3072,768]{1,0:T(8,128)(2,1)} fusion(bf16[1176,3072]{1,0:T(8,128)(2,1)} %get-tuple-element.252, bf16[1176,768]{1,0:T(8,128)(2,1)S(1)} %copy-done.15, f32[1176]{0:T(1024)S(1)} %copy-done.19), kind=kOutput, calls=%fused_computation.78 | convolution fusion | flops 5554132992 | bytes 13754976 | tf_op jit(solution)/shard_map/dot_general | solution.py:72
  311.8 3.7 convolution_convert_fusion.4
  315.4 6.8 reshape.303
  322.2 9.3 %copy.97 = bf16[3,8,49,24,32]{2,4,3,1,0:T(8,128)(2,1)} copy(bf16[3,8,49,24,32]{4,3,2,1,0:T(8,128)(2,1)} %reshape.303) | data formatting | bytes 3612672
  331.5 11.9 %convolution_convert_fusion.2 = bf16[768,3072]{1,0:T(8,128)(2,1)} fusion(bf16[1176,3072]{1,0:T(8,128)(2,1)} %get-tuple-element.272, f32[1176,768]{1,0:T(8,128)} %copy-done.10, f32[768]{0:T(1024)S(1)} %copy-done.36, f32[768]{0:T(1024)S(1)} %copy-done.23, f32[1176]{0:T(1024)S(1)} %add_rsqrt_fusion, f32[1176]{0:T(1024)S(1)} %broadcast_multiply_fusion.4), kind=kOutput, calls=%fused_computation.79 | convolution fusion | flops 5555939328 | bytes 15572160 | tf_op jit(solution)/shard_map/dot_general | solution.py:72
  344.4 130.9 %while.26 = (s32[]{:T(128)}, f32[24,49,49]{1,2,0:T(8,128)}, bf16[3,392,2304]{1,2,0:T(8,128)(2,1)}, f32[3,8,49,24,3,32]{2,5,3,1,4,0:T(8,128)}, f32[24,2401]{1,0:T...) while((s32[]{:T(128)}, f32[24,49,49]{1,2,0:T(8,128)}, ...), condition=%wide.region_16.17_spmd.clone, body=%wide.region_13.16_spmd.clone.sunk | while | flops 160520480 | bytes 74468408 | solution.py:151
  347.8 7.6 fusion.131
  355.5 3.1 fusion.132
  358.6 3.2 fusion.133
  361.8 4.0 multiply_reduce_fusion.8
  372.4 7.7 copy.124
  380.1 6.4 convert_element_type.349
  391.2 8.1 fusion.131
  402.4 3.2 fusion.133
  405.6 4.0 multiply_reduce_fusion.8
  416.2 7.7 copy.124
  423.9 6.4 convert_element_type.349
  434.9 7.7 fusion.131
  445.7 3.2 fusion.133
  448.9 4.0 multiply_reduce_fusion.8
  459.5 7.7 copy.124
  467.1 6.4 convert_element_type.349
  475.4 9.1 %copy.98 = bf16[3,392,2304]{2,1,0:T(8,128)(2,1)} copy(bf16[3,392,2304]{1,2,0:T(8,128)(2,1)} %get-tuple-element.93) | data formatting | bytes 10838016 | tf_op jit(solution)/shard_map/while | solution.py:151
  484.5 9.2 %convolution_convert_fusion.3 = bf16[768,2304]{1,0:T(8,128)(2,1)} fusion(bf16[1176,2304]{1,0:T(8,128)(2,1)} %bitcast.156, bf16[1176,768]{1,0:T(8,128)(2,1)S(1)} %copy-done.9, f32[768]{0:T(1024)S(1)} %copy-done.35, f32[768]{0:T(1024)S(1)} %copy-done.25, f32[1176]{0:T(1024)S(1)} %copy-done.22, f32[1176]{0:T(1024)S(1)} %copy-done.18), kind=kOutput, calls=%fused_computation.80 | convolution fusion | flops 4168986624 | bytes 10779840 | tf_op jit(solution)/shard_map/dot_general | solution.py:72
  493.7 5.8 copy.108
  499.7 10.6 %fusion.65 = (bf16[768]{0:T(1024)(128)(2,1)S(1)}, f32[1176]{0:T(1024)S(1)}, f32[1176]{0:T(1024)S(1)}, bf16[768]{0:T(1024)(128)(2,1)S(1)}, f32[1176,768]{1,0:T(8,128)}) fusion(bf16[1176,768]{1,0:T(8,128)(2,1)S(1)} %copy-done.9, f32[1176]{0:T(1024)S(1)} %copy-done.22, f32[1176]{0:T(1024)S(1)} %copy-done.18, f32[768]{0:T(1024)S(1)} %copy-done.25, ...), kind=kOutput, calls=%fused_computation.102 | convolution fusion | flops 4170825728 | bytes 14401920 | tf_op jit(solution)/shard_map/dot_general | solution.py:78
  511.9 36.1 %reduce-scatter.20.cloned.1.call-done = bf16[1152,768]{1,0:T(8,128)(2,1)} async-done(((bf16[2304,768]{1,0:T(8,128)(2,1)}), bf16[1152,768]{1,0:T(8,128)(2,1)}) %reduce-scatter.20.cloned.1.call-update) | async-done | bytes 1769488
  548.0 3.9 copy.109
  554.5 4.2 reduce.3
  560.2 5.3 fusion
  565.5 3.7 collective-permute-start
  569.3 6.9 all-reduce.6
  576.3 5.5 fusion.64
  581.8 10.5 %fusion.67 = bf16[1176,768]{1,0:T(8,128)(2,1)} fusion(f32[1176,768]{1,0:T(8,128)S(1)} %copy-done.12, bf16[1176,3072]{1,0:T(8,128)(2,1)} %get-tuple-element.252, bf16[3072,768]{1,0:T(8,128)(2,1)} %all-gather.15.cloned.1.call-done, f32[768]{0:T(1024)S(1)} %convert_element_type.201, f32[1176]{0:T(1024)S(1)} %copy-done.20), kind=kOutput, calls=%fused_computation.111 | convolution fusion | flops 5552676864 | bytes 17370720 | tf_op jit(solution)/shard_map/dot_general | solution.py:214
  593.6 58.9 %all-reduce.4 = (bf16[6,384]{1,0:T(8,128)(2,1)S(1)}, bf16[12,2,32]{2,1,0:T(2,128)(2,1)S(1)}, bf16[12,169]{1,0:T(8,128)(2,1)S(1)}, bf16[1536]{0:T(1024)(128)(2,1)S(1)}) all-reduce(bf16[6,384]{1,0:T(8,128)(2,1)S(1)} %copy.107, bf16[12,2,32]{2,1,0:T(2,128)(2,1)S(1)} %constant_dynamic-slice_fusion.1, ...), channel_id=1, replica_groups=mesh['dp'=16,'tensor'=2] {'dp'}, use_global_device_ids=true, to_apply=%region_26.27 | all-reduce | flops 6636 | bytes 26544 | tf_op jit(solution)/shard_map/psum | solution.py:306
  655.0 36.2 %all-reduce.9.cloned.1.call-done = (bf16[384,768]{1,0:T(8,128)(2,1)}, bf16[768,1536]{1,0:T(8,128)(2,1)}, bf16[1536,768]{1,0:T(8,128)(2,1)}) async-done(((bf16[384,768]{1,0:T(8,128)(2,1)}, bf16[768,1536]{1,0:T(8,128)(2,1)}, bf16[1536,768]{1,0:T(8,128)(2,1)}), (bf16[384,768]{1,0:T(8,128)(2,1)}, bf16[768,1536]{1,0:T(8,128)(2,1)}, bf16[1536,768]{1,0:T(8,128)(2,1)})) %all-reduce.9.cloned.1.call-update) | async-done | bytes 5308432 | tf_op jit(solution)/shard_map/psum | solution.py:302
  693.4 4.6 convert_element_type.218
  700.7 136.3 %all-gather.17.cloned.1.call-done = bf16[12288,1152]{1,0:T(8,128)(2,1)} async-done(((bf16[768,1152]{1,0:T(8,128)(2,1)}), bf16[12288,1152]{1,0:T(8,128)(2,1)}) %all-gather.17.cloned.1.call-update) | async-done | bytes 28311568 | tf_op jit(solution)/shard_map/all_gather | solution.py:15
  837.0 10.1 %reduce_sum.210 = bf16[768,1152]{1,0:T(8,128)(2,1)S(1)} reduce(bf16[16,768,1152]{2,1,0:T(8,128)(2,1)} %bitcast.154, bf16[]{:T(256)} %constant.57.clone.1), dimensions={0}, to_apply=%region_28.29 | reduce | flops 13271040 | bytes 30081026 | tf_op jit(solution)/shard_map/reduce_sum | solution.py:16
  (280 shorter events, 94.0 us)
Async XLA Ops:
  7.2 3.0 copy-start.50
  7.2 3.7 copy-start.39
  7.2 3.7 copy-start.40
  7.2 4.3 copy-start.41
  7.2 4.3 copy-start.42
  7.2 4.9 copy-start.43
  7.2 5.5 copy-start.38
  7.3 11.3 %copy-start.8 = (bf16[1176,768]{1,0:T(8,128)(2,1)S(1)}, bf16[1176,768]{1,0:T(8,128)(2,1)}, u32[]{:S(2)}) copy-start(bf16[1176,768]{1,0:T(8,128)(2,1)} %param.20) | copy-start | bytes 5419012
  7.3 54.7 %all-gather.9.cloned.1.call-start = ((), (), s32[]{:S(2)}) async-start(), calls=%async_computation.5 | async-start | bytes 5308416 | tf_op jit(solution)/shard_map/all_gather | solution.py:187
  8.0 202.2 %all-gather.11.cloned.1.call-start = ((), (), s32[]{:S(2)}) async-start(), calls=%async_computation.6 | async-start | bytes 1769472 | tf_op jit(solution)/shard_map/all_gather | solution.py:190
  8.7 208.2 %all-gather.13.cloned.1.call-start = ((), (), s32[]{:S(2)}) async-start(), calls=%async_computation.7 | async-start | bytes 7077888 | tf_op jit(solution)/shard_map/all_gather | solution.py:191
  9.5 10.8 %copy-start.32 = (bf16[12,2,32]{2,1,0:T(2,128)(2,1)S(1)}, bf16[12,2,32]{2,1,0:T(2,128)(2,1)}, u32[]{:S(2)}) copy-start(bf16[12,2,32]{2,1,0:T(2,128)(2,1)} %param.24) | copy-start | bytes 4612
  9.5 15.2 %copy-start.31 = (bf16[12,169]{1,0:T(8,128)(2,1)S(1)}, bf16[12,169]{1,0:T(8,128)(2,1)}, u32[]{:S(2)}) copy-start(bf16[12,169]{1,0:T(8,128)(2,1)} %param.25) | copy-start | bytes 12172
  9.5 248.5 %all-gather.15.cloned.1.call-start = ((), (), s32[]{:S(2)}) async-start(), calls=%async_computation.8 | async-start | bytes 7077888 | tf_op jit(solution)/shard_map/all_gather | solution.py:193
  10.1 501.2 %reduce-scatter.12.cloned.1.call-start = ((), (), s32[]{:S(2)}) async-start(), calls=%async_computation.9 | async-start | bytes 1769472 | tf_op jit(solution)/shard_map/reduce_scatter | solution.py:282
  10.9 60.5 %copy-start.24 = (f32[768]{0:T(1024)}, f32[768]{0:T(1024)S(1)}, u32[]{:S(2)}) copy-start(f32[768]{0:T(1024)S(1)} %convert_element_type.190) | copy-start | bytes 9220
  11.5 59.9 %copy-start.34 = (f32[768]{0:T(1024)}, f32[768]{0:T(1024)S(1)}, u32[]{:S(2)}) copy-start(f32[768]{0:T(1024)S(1)} %convert_element_type.191) | copy-start | bytes 9220
  18.9 52.5 %copy-start.17 = (f32[1176]{0:T(1024)}, f32[1176]{0:T(1024)S(1)}, u32[]{:S(2)}) copy-start(f32[1176]{0:T(1024)S(1)} %broadcast_multiply_fusion.5) | copy-start | bytes 14116
  19.6 51.8 %copy-start.21 = (f32[1176]{0:T(1024)}, f32[1176]{0:T(1024)S(1)}, u32[]{:S(2)}) copy-start(f32[1176]{0:T(1024)S(1)} %add_rsqrt_fusion.1) | copy-start | bytes 14116
  29.8 41.7 %copy-start.27 = (s32[2401]{0:T(1024)}, s32[2401]{0:T(1024)S(1)}, u32[]{:S(2)}) copy-start(s32[2401]{0:T(1024)S(1)} %reshape.296) | copy-start | bytes 28816
  132.0 78.2 %copy-start.19 = (f32[1176]{0:T(1024)S(1)}, f32[1176]{0:T(1024)}, u32[]{:S(2)}) copy-start(f32[1176]{0:T(1024)} %mul.191) | copy-start | bytes 14116
  132.0 78.2 %copy-start.37 = (f32[768]{0:T(1024)S(1)}, f32[768]{0:T(1024)}, u32[]{:S(2)}) copy-start(f32[768]{0:T(1024)} %convert_element_type.195) | copy-start | bytes 9220
  141.2 3.9 copy-start.2
  167.9 4.0 copy-start.2
  193.6 3.9 copy-start.2
  210.1 4.4 copy-start.6
  210.2 4.4 copy-start.16
  214.5 2.4 copy-start.23
  214.6 2.4 copy-start.26
  214.6 2.4 copy-start.36
  217.0 41.1 %copy-start.15 = (bf16[1176,768]{1,0:T(8,128)(2,1)S(1)}, bf16[1176,768]{1,0:T(8,128)(2,1)}, u32[]{:S(2)}) copy-start(bf16[1176,768]{1,0:T(8,128)(2,1)} %param.35) | copy-start | bytes 5419012
  277.5 13.2 %copy-start.11 = (f32[1176,768]{1,0:T(8,128)S(1)}, f32[1176,768]{1,0:T(8,128)}, u32[]{:S(2)}) copy-start(f32[1176,768]{1,0:T(8,128)} %copy-done.10) | copy-start | bytes 10838020
  290.7 4.5 copy-start.48
  293.4 1.8 copy-start.13
  298.3 213.0 %reduce-scatter.16.cloned.1.call-start = ((), (), s32[]{:S(2)}) async-start(), calls=%async_computation.11 | async-start | bytes 7077888 | tf_op jit(solution)/shard_map/reduce_scatter | solution.py:291
  310.5 200.8 %reduce-scatter.14.cloned.1.call-start = ((), (), s32[]{:S(2)}) async-start(), calls=%async_computation.10 | async-start | bytes 7077888 | tf_op jit(solution)/shard_map/reduce_scatter | solution.py:285
  343.5 204.5 %reduce-scatter.20.cloned.1.call-start = ((), (), s32[]{:S(2)}) async-start(), calls=%async_computation.14 | async-start | bytes 5308416
  355.5 3.1 copy-start.1
  358.6 3.2 copy-start
  399.3 3.1 copy-start.1
  402.4 3.2 copy-start
  442.6 3.1 copy-start.1
  445.7 3.2 copy-start
  475.3 9.2 %copy-start.9 = (bf16[1176,768]{1,0:T(8,128)(2,1)S(1)}, bf16[1176,768]{1,0:T(8,128)(2,1)}, u32[]{:S(2)}) copy-start(bf16[1176,768]{1,0:T(8,128)(2,1)} %param.20) | copy-start | bytes 5419012
  475.3 9.2 %copy-start.18 = (f32[1176]{0:T(1024)S(1)}, f32[1176]{0:T(1024)}, u32[]{:S(2)}) copy-start(f32[1176]{0:T(1024)} %copy-done.17) | copy-start | bytes 14116
  475.3 9.2 %copy-start.22 = (f32[1176]{0:T(1024)S(1)}, f32[1176]{0:T(1024)}, u32[]{:S(2)}) copy-start(f32[1176]{0:T(1024)} %copy-done.21) | copy-start | bytes 14116
  475.3 9.2 %copy-start.25 = (f32[768]{0:T(1024)S(1)}, f32[768]{0:T(1024)}, u32[]{:S(2)}) copy-start(f32[768]{0:T(1024)} %copy-done.24) | copy-start | bytes 9220
  475.4 9.2 %copy-start.35 = (f32[768]{0:T(1024)S(1)}, f32[768]{0:T(1024)}, u32[]{:S(2)}) copy-start(f32[768]{0:T(1024)} %copy-done.34) | copy-start | bytes 9220
  493.7 5.9 copy-start.46
  493.7 5.9 copy-start.45
  493.7 5.9 copy-start.30
  493.7 6.0 copy-start.29
  499.5 93.1 %reduce-scatter.18.cloned.1.call-start = ((), (), s32[]{:S(2)}) async-start(), calls=%async_computation.13 | async-start | bytes 294912
  511.2 180.0 %all-reduce.9.cloned.1.call-start = ((), (), s32[]{:S(2)}) async-start(), calls=%async_computation.15 | async-start | bytes 10616832 | tf_op jit(solution)/shard_map/psum | solution.py:302
  511.8 40.1 %copy-start.47 = (u32[32]{0:T(128)S(1)}, u32[32]{0:T(128)}, u32[]{:S(2)}) copy-start(u32[32]{0:T(128)} %constant.183) | copy-start | bytes 388
  511.8 42.6 %copy-start.44 = (bf16[768]{0:T(1024)(128)(2,1)S(1)}, bf16[768]{0:T(1024)(128)(2,1)}, u32[]{:S(2)}) copy-start(bf16[768]{0:T(1024)(128)(2,1)} %param.33) | copy-start | bytes 4612
  511.8 325.2 %all-gather.17.cloned.1.call-start = ((), (), s32[]{:S(2)}) async-start(), calls=%async_computation.12 | async-start | bytes 30081024 | tf_op jit(solution)/shard_map/all_gather | solution.py:15
  551.8 6.8 copy-start.5
  554.4 4.8 copy-start.28
  554.4 14.9 %copy-start.33 = (bf16[3072]{0:T(1024)(128)(2,1)S(1)}, bf16[3072]{0:T(1024)(128)(2,1)}, u32[]{:S(2)}) copy-start(bf16[3072]{0:T(1024)(128)(2,1)} %get-tuple-element.271) | copy-start | bytes 18436
  565.5 27.0 %collective-permute-start = (bf16[4,169]{1,0:T(4,128)(2,1)S(1)}, bf16[4,169]{1,0:T(4,128)(2,1)S(1)}, u32[]{:S(2)}, u32[]{:S(2)}) collective-permute-start(bf16[4,169]{1,0:T(4,128)(2,1)S(1)} %slice.83), channel_id=1, source_target_pairs={{0,1},{2,3},{4,5},{6,7},{8,9},{10,11},{12,13},{14,15},{16,17},{18,... | collective-permute-start | bytes 4064
  576.3 5.6 copy-start.12
  576.3 5.6 copy-start.20
  693.4 4.7 copy-start.14
  (9 other events, 11.1 us)
Sparse Core Ops, SparseCore 0:
  9.6 52.2 all-gather.8
  63.5 22.8 all-gather.10
  87.9 62.6 all-gather.12
  152.0 62.6 all-gather.14
  298.4 22.0 reduce-scatter.11
  322.7 59.9 reduce-scatter.15
  385.6 59.9 reduce-scatter.13
  499.6 48.2 reduce-scatter.19
  550.2 10.9 reduce-scatter.17
  565.1 126.0 all-reduce.8
  693.5 143.4 all-gather.16
